TPU v7x, 256 devices: a whole 4x4x8 slice. The times are simulated.
256 devices in a mesh: row: 8 (over x, core), col: 32 (over z, y).
Axes of the slice: x: 4, y: 4, z: 8, core: 2. Of those that a mesh axis runs over, the one named last changes fastest.
Arguments:
- matrix: float32 [24576, 12288], P('row', 'col'), may hold values from -6 to 6
Outputs:
- updated: float32 [24576, 12288], P('row', 'col')
All inputs are finite; a program needn't handle non-finite values.
Results may differ from a plain program's by a relative error of at most 0.0003.
Values sent between devices are 32-bit elements; how exact they have to be, the bound alone decides.
A program may use at most 64 MiB of HBM per device.

v0:
```python
import jax
import jax.numpy as jnp
from jax import lax
from jax.sharding import PartitionSpec as P

PANEL = 256


HIGHEST = lax.Precision.HIGHEST


def partner_2(block, axis, distance):
    count = lax.axis_size(axis)
    route = []
    for low in range(count):
        high = low | 1 << distance
        if high != low and high < count:
            route += [(low, high), (high, low)]
    return lax.ppermute(block, axis, route)


def broadcast(value, axis, source):
    kept = jnp.where(lax.axis_index(axis) == source, value, 0).astype(value.dtype)
    return lax.psum(kept, axis)


def upper_of(gram):
    return jnp.linalg.cholesky(gram).T


def combine_pair(upper_one, upper_two):
    gram = jnp.dot(upper_one.T, upper_one, precision=HIGHEST) + jnp.dot(
        upper_two.T, upper_two, precision=HIGHEST
    )
    return upper_of(gram)


def apply_inverse(upper, rows):
    return jax.scipy.linalg.solve_triangular(upper.T, rows.T, lower=True).T


def factor(panel):
    gram_local = lax.dot_general(panel, panel, (((0,), (0,)), ((), ())), precision=HIGHEST)
    is_first = lax.axis_index("row") == 0
    identity = jnp.eye(PANEL, dtype=jnp.float32)
    upper = upper_of(gram_local)
    for level in range(lax.axis_size("row").bit_length() - 1):
        partner = partner_2(upper, "row", level)
        upper = combine_pair(upper, partner)
    basis = apply_inverse(upper, panel)
    top_block = broadcast(basis[:PANEL], "row", 0)
    lead = identity + top_block
    vectors = basis.at[:PANEL].add(jnp.where(is_first, identity, jnp.zeros_like(identity)))
    return (vectors, lead)


def on_device(matrix):
    panel = matrix[:, :PANEL]
    vectors, lead = factor(panel)
    vectors, lead = (broadcast(vectors, "col", 0), broadcast(lead, "col", 0))
    partial_proj = lax.dot_general(vectors, matrix, (((0,), (0,)), ((), ())), precision=HIGHEST)
    projected = lax.psum(partial_proj, "row")
    lead_gram = jnp.dot(lead.T, lead, precision=HIGHEST)
    lead_factor = jnp.linalg.cholesky(lead_gram)
    coeffs = jax.scipy.linalg.cho_solve(
        (lead_factor, True), jnp.dot(lead.T, projected, precision=HIGHEST)
    )
    return matrix - jnp.dot(vectors, coeffs, precision=HIGHEST)


def solution(mesh):
    in_specs = (P("row", "col"),)
    out_specs = P("row", "col")
    return jax.shard_map(
        on_device, mesh=mesh, in_specs=in_specs, out_specs=out_specs, check_vma=False
    )
```

profile of v0, /device:TPU:8, one launch (start us, length us, event | category | flops | bytes accessed | tf_op | source)
XLA Modules:
  0.0 583.5 jit_solution(9986484635231155321)
XLA Ops:
  6.5 7.9 %fusion.1 = f32[256,256]{1,0:T(8,128)S(1)} fusion(f32[3072,384]{1,0:T(8,128)} %param.4), kind=kOutput, calls=%fused_computation.11 | convolution fusion | flops 2415919104 | bytes 3407872 | tf_op jit(solution)/shard_map/dot_general | solution.py:43
  14.7 11.7 %cholesky.256 = f32[128,128]{1,0:T(8,128)S(1)} custom-call(f32[128,128]{1,0:T(8,128)S(1)} %cholesky.422), custom_call_target="Cholesky" | custom-call | tf_op jit(solution)/shard_map/jit(cholesky)/cholesky | solution.py:28
  26.4 9.8 %custom-call.25 = f32[1,128,128]{1,2,0:T(8,128)S(1)} custom-call(f32[1,128,128]{2,1,0:T(8,128)S(1)} %get-tuple-element.77), custom_call_target="InvertDiagBlocksLowerTriangular" | custom-call | tf_op jit(solution)/shard_map/jit(cholesky)/cholesky | solution.py:28
  36.8 11.9 %cholesky.273 = f32[128,128]{1,0:T(8,128)S(1)} custom-call(f32[128,128]{1,0:T(8,128)S(1)} %convolution_subtract_fusion.5), custom_call_target="Cholesky" | custom-call | tf_op jit(solution)/shard_map/jit(cholesky)/cholesky | solution.py:28
  48.7 0.7 compare_reduce_fusion.8
  51.3 1.1 collective-permute-done
  53.0 11.7 %cholesky.290 = f32[128,128]{1,0:T(8,128)S(1)} custom-call(f32[128,128]{1,0:T(8,128)S(1)} %cholesky.425), custom_call_target="Cholesky" | custom-call | tf_op jit(solution)/shard_map/jit(cholesky)/cholesky | solution.py:28
  64.8 9.8 %custom-call.26 = f32[1,128,128]{1,2,0:T(8,128)S(1)} custom-call(f32[1,128,128]{2,1,0:T(8,128)S(1)} %get-tuple-element.73), custom_call_target="InvertDiagBlocksLowerTriangular" | custom-call | tf_op jit(solution)/shard_map/jit(cholesky)/cholesky | solution.py:28
  75.1 11.7 %cholesky.307 = f32[128,128]{1,0:T(8,128)S(1)} custom-call(f32[128,128]{1,0:T(8,128)S(1)} %slice_subtract_fusion.2), custom_call_target="Cholesky" | custom-call | tf_op jit(solution)/shard_map/jit(cholesky)/cholesky | solution.py:28
  86.8 0.7 compare_reduce_fusion.6
  87.6 0.6 compare_reduce_fusion.7
  89.6 2.0 collective-permute-start.1
  91.6 3.8 slice_bitcast_fusion
  95.7 2.7 collective-permute-done.1
  99.0 11.7 %cholesky.324 = f32[128,128]{1,0:T(8,128)S(1)} custom-call(f32[128,128]{1,0:T(8,128)S(1)} %cholesky.428), custom_call_target="Cholesky" | custom-call | tf_op jit(solution)/shard_map/jit(cholesky)/cholesky | solution.py:28
  110.8 9.8 %custom-call.27 = f32[1,128,128]{1,2,0:T(8,128)S(1)} custom-call(f32[1,128,128]{2,1,0:T(8,128)S(1)} %get-tuple-element.69), custom_call_target="InvertDiagBlocksLowerTriangular" | custom-call | tf_op jit(solution)/shard_map/jit(cholesky)/cholesky | solution.py:28
  121.1 11.7 %cholesky.341 = f32[128,128]{1,0:T(8,128)S(1)} custom-call(f32[128,128]{1,0:T(8,128)S(1)} %slice_subtract_fusion.1), custom_call_target="Cholesky" | custom-call | tf_op jit(solution)/shard_map/jit(cholesky)/cholesky | solution.py:28
  132.8 0.6 compare_reduce_fusion.4
  133.5 0.7 compare_reduce_fusion.5
  135.5 3.3 collective-permute-start.2
  139.2 5.6 collective-permute-done.2
  145.3 11.7 %cholesky.358 = f32[128,128]{1,0:T(8,128)S(1)} custom-call(f32[128,128]{1,0:T(8,128)S(1)} %cholesky.431), custom_call_target="Cholesky" | custom-call | tf_op jit(solution)/shard_map/jit(cholesky)/cholesky | solution.py:28
  157.1 9.8 %custom-call.28 = f32[1,128,128]{1,2,0:T(8,128)S(1)} custom-call(f32[1,128,128]{2,1,0:T(8,128)S(1)} %get-tuple-element.65), custom_call_target="InvertDiagBlocksLowerTriangular" | custom-call | tf_op jit(solution)/shard_map/jit(cholesky)/cholesky | solution.py:28
  167.4 11.7 %cholesky.375 = f32[128,128]{1,0:T(8,128)S(1)} custom-call(f32[128,128]{1,0:T(8,128)S(1)} %slice_subtract_fusion), custom_call_target="Cholesky" | custom-call | tf_op jit(solution)/shard_map/jit(cholesky)/cholesky | solution.py:28
  179.2 0.7 compare_reduce_fusion.2
  179.8 0.6 compare_reduce_fusion.3
  181.8 4.0 while.3
  182.6 1.3 bitcast_dynamic-update-slice_fusion.4
  184.5 1.3 bitcast_dynamic-update-slice_fusion.4
  185.8 19.7 %custom-call.19 = f32[2,128,128]{1,2,0:T(8,128)S(1)} custom-call(f32[2,128,128]{2,1,0:T(8,128)S(1)} %get-tuple-element.25), custom_call_target="InvertDiagBlocksLowerTriangular" | custom-call | tf_op jit(solution)/shard_map/jit(_solve_triangular)/triangular_solve | solution.py:39
  205.5 2.9 fusion.3
  208.4 5.2 convolution_subtract_fusion.1
  214.0 2.8 fusion.38
  217.1 0.8 slice_select_fusion
  217.9 1.7 copy-done
  219.6 1.9 broadcast_select_fusion
  221.5 66.5 %all-reduce.6.cloned.1.call-done = f32[256,256]{1,0:T(8,128)} async-done(((f32[256,256]{1,0:T(8,128)}), f32[256,256]{1,0:T(8,128)}) %all-reduce.6.cloned.1.call-update) | async-done | bytes 262160 | tf_op jit(solution)/shard_map/psum | solution.py:24
  287.9 1.7 fusion.10
  290.1 159.1 %all-reduce.10.cloned.1.call-done = (f32[3072,256]{1,0:T(8,128)}, f32[256,256]{1,0:T(8,128)}) async-done(((f32[3072,256]{1,0:T(8,128)}, f32[256,256]{1,0:T(8,128)}), (f32[3072,256]{1,0:T(8,128)}, f32[256,256]{1,0:T(8,128)})) %all-reduce.10.cloned.1.call-update) | async-done | bytes 3407888 | tf_op jit(solution)/shard_map/psum | solution.py:24
  449.2 1.8 fusion.78
  451.0 0.8 copy.14
  451.9 1.0 fusion.13
  452.9 0.7 copy-done.4
  453.6 11.7 %cholesky.392 = f32[128,128]{1,0:T(8,128)S(1)} custom-call(f32[128,128]{1,0:T(8,128)S(1)} %cholesky.434), custom_call_target="Cholesky" | custom-call | tf_op jit(solution)/shard_map/jit(cholesky)/cholesky | solution.py:64
  465.3 9.8 %custom-call.29 = f32[1,128,128]{1,2,0:T(8,128)S(1)} custom-call(f32[1,128,128]{2,1,0:T(8,128)S(1)} %get-tuple-element.61), custom_call_target="InvertDiagBlocksLowerTriangular" | custom-call | tf_op jit(solution)/shard_map/jit(cholesky)/cholesky | solution.py:64
  475.1 1.0 constant_dynamic-update-slice_fusion.1
  476.2 1.1 convolution_subtract_fusion.4
  477.3 11.7 %cholesky.409 = f32[128,128]{1,0:T(8,128)S(1)} custom-call(f32[128,128]{1,0:T(8,128)S(1)} %convolution_subtract_fusion.4), custom_call_target="Cholesky" | custom-call | tf_op jit(solution)/shard_map/jit(cholesky)/cholesky | solution.py:64
  489.1 0.7 compare_reduce_fusion
  489.8 0.7 compare_reduce_fusion.1
  490.5 8.0 %fusion.79 = f32[256,384]{1,0:T(8,128)} fusion(f32[3072,256]{1,0:T(8,128)S(1)} %copy-done.1, f32[3072,384]{1,0:T(8,128)} %param.4), kind=kOutput, calls=%fused_computation.151 | convolution fusion | flops 3623878656 | bytes 8257536 | tf_op jit(solution)/shard_map/dot_general | solution.py:61
  499.8 1.7 select_select_fusion
  501.5 5.7 while.4
  501.5 0.6 fusion.114
  502.1 2.2 bitcast_dynamic-update-slice_fusion.5
  504.4 0.6 fusion.114
  505.0 2.2 bitcast_dynamic-update-slice_fusion.5
  507.2 0.6 copy-done.5
  507.8 20.5 %custom-call.20 = f32[2,128,128]{1,2,0:T(8,128)S(1)} custom-call(f32[2,128,128]{2,1,0:T(8,128)} %copy-done.5), custom_call_target="InvertDiagBlocksLowerTriangular" | custom-call | tf_op jit(solution)/shard_map/jit(_cho_solve)/triangular_solve | solution.py:65
  528.3 34.7 %all-reduce.8.cloned.1.call-done = f32[256,384]{1,0:T(8,128)} async-done(((f32[256,384]{1,0:T(8,128)}), f32[256,384]{1,0:T(8,128)}) %all-reduce.8.cloned.1.call-update) | async-done | bytes 393232 | tf_op jit(solution)/shard_map/psum | solution.py:62
  563.0 1.6 fusion.80
  565.0 1.2 convolution_subtract_fusion.3
  566.9 1.2 convolution_subtract_fusion.2
  568.4 8.4 %convolution_subtract_fusion = f32[3072,384]{1,0:T(8,128)} fusion(f32[3072,384]{1,0:T(8,128)} %param.4, f32[3072,256]{1,0:T(8,128)S(1)} %copy-done.1, f32[128,384]{1,0:T(8,128)S(1)} %fusion.65, f32[128,384]{1,0:T(8,128)S(1)} %fusion.64), kind=kOutput, calls=%fused_computation.4 | convolution fusion | flops 3625156608 | bytes 12976128 | tf_op jit(solution)/shard_map/dot_general | solution.py:68
  (78 shorter events, 9.6 us)
Async XLA Ops:
  6.5 281.4 %all-reduce.6.cloned.1.call-start = ((), (), s32[]{:S(2)}) async-start(), calls=%async_computation | async-start | bytes 524288 | tf_op jit(solution)/shard_map/psum | solution.py:24
  50.8 1.6 collective-permute-start
  89.6 8.8 %collective-permute-start.1 = (f32[256,256]{0,1:T(8,128)S(1)}, f32[256,256]{0,1:T(8,128)S(1)}, u32[]{:S(2)}, u32[]{:S(2)}) collective-permute-start(f32[256,256]{0,1:T(8,128)S(1)} %fusion.20), channel_id=1, source_target_pairs={{0,64},{64,0},{32,96},{96,32},{128,192},{192,128},{160,224},{224,1... | collective-permute-start | bytes 786440 | tf_op jit(solution)/shard_map/ppermute | solution.py:19
  135.5 9.3 %collective-permute-start.2 = (f32[256,256]{0,1:T(8,128)S(1)}, f32[256,256]{0,1:T(8,128)S(1)}, u32[]{:S(2)}, u32[]{:S(2)}) collective-permute-start(f32[256,256]{0,1:T(8,128)S(1)} %fusion.22), channel_id=1, source_target_pairs={{0,128},{128,0},{32,160},{160,32},{64,192},{192,64},{96,224},{224,... | collective-permute-start | bytes 786440 | tf_op jit(solution)/shard_map/ppermute | solution.py:19
  217.9 1.7 copy-start
  219.5 229.7 %all-reduce.10.cloned.1.call-start = ((), (), s32[]{:S(2)}) async-start(), calls=%async_computation.2 | async-start | bytes 6815744 | tf_op jit(solution)/shard_map/psum | solution.py:24
  289.7 273.3 %all-reduce.8.cloned.1.call-start = ((), (), s32[]{:S(2)}) async-start(), calls=%async_computation.1 | async-start | bytes 786432 | tf_op jit(solution)/shard_map/psum | solution.py:62
  449.2 41.2 %copy-start.1 = (f32[3072,256]{1,0:T(8,128)S(1)}, f32[3072,256]{1,0:T(8,128)}, u32[]{:S(2)}) copy-start(f32[3072,256]{1,0:T(8,128)} %get-tuple-element.50) | copy-start | bytes 9437188
  452.8 0.7 copy-start.4
  489.1 1.4 copy-start.3
  490.5 72.5 %copy-start.2 = (f32[256,256]{1,0:T(8,128)S(1)}, f32[256,256]{1,0:T(8,128)}, u32[]{:S(2)}) copy-start(f32[256,256]{1,0:T(8,128)} %get-tuple-element.51) | copy-start | bytes 786436
  507.2 0.6 copy-start.5
Sparse Core Ops, SparseCore 0:
  219.7 68.2 all-reduce.5
  291.6 157.5 all-reduce.9
  498.6 64.3 all-reduce.7
where the time goes:
time: 593 us; the launch traced here: 583 us
  waiting for transfers between devices  270 us (46%)
  other arithmetic  220 us (37%)
  matrix products  48.8 us (8%)
  between operations  20.2 us (3%)
  local copies, waits for them, and re-layouts  18.1 us (3%)
    psum x2, waiting for transfers between devices, broadcast(): return lax.psum(kept, axis)  226 us
    another operation x27, other arithmetic, upper_of(): return jnp.linalg.cholesky(gram).T  138 us
    another operation x7, other arithmetic, on_device(): lead_factor = jnp.linalg.cholesky(lead_gram)  34.7 us
    psum x1, waiting for transfers between devices, on_device(): projected = lax.psum(partial_proj, 'row')  34.7 us
    another operation x2, other arithmetic, on_device(): jax.scipy.linalg.cho_solve((lead_factor, True), jnp.dot(lead.T, projected...  22.2 us
    another operation x3, other arithmetic, apply_inverse(): return jax.scipy.linalg.solve_triangular(upper.T, rows.T, lower=True).T  19.7 us
  transfers between devices with their start and end apart: 6, of which 6 were waited for; matrix products, arithmetic and copies ran while one was open for 6% of the time, Pallas kernels for 0%

commit v1 on v0

v1 whole, which is shorter than its diff:
```python
import functools

import jax
import jax.numpy as jnp
from jax import lax
from jax.experimental import pallas as pl
from jax.experimental.pallas import tpu as pltpu
from jax.sharding import PartitionSpec as P

PANEL = 256
Y, Z = 4, 8
ROW = 8
PIECE = 32
BLOCK = 64
MESH = pl.DeviceIdType.MESH
HIGHEST = lax.Precision.HIGHEST

TREES = (
    (205809287, 1078206464, 153162274, 1145052164),
    (2425421888, 2348828425, 538199108, 2291729160),
    (1646792752, 573083664, 1082827025, 536928418),
    (16943360, 294848740, 2252343432, 321257537),
)
DEPTHS = (
    (1515870810, 3552543676, 3221224912),
    (1515870810, 3647453556, 671088562),
    (1515870810, 2381649390, 4294962692),
    (1515870810, 3474847550, 1693450230),
)
LAG = 4


def signed(mask):
    return mask - (1 << 32) if mask >= 1 << 31 else mask


def passes(tree, direction, col):
    return (jnp.int32(signed(TREES[tree][direction])) >> col) & 1 == 1


def neighbour(col, direction):
    y, z = lax.rem(col, Y), lax.div(col, Y)
    if direction == 0:
        y = lax.rem(y + 1, Y)
    elif direction == 1:
        y = lax.rem(y + Y - 1, Y)
    elif direction == 2:
        z = lax.rem(z + 1, Z)
    else:
        z = lax.rem(z + Z - 1, Z)
    return z * Y + y


def dot_t(a, b):
    return lax.dot_general(
        a, b, (((0,), (0,)), ((), ())), precision=HIGHEST, preferred_element_type=jnp.float32
    )


def dot(a, b):
    return jnp.dot(a, b, precision=HIGHEST, preferred_element_type=jnp.float32)


def tree_send(buf, send_sems, recv_sems, tree, direction, index, rows, col):
    row = lax.axis_index("row")
    return pltpu.make_async_remote_copy(
        src_ref=buf.at[rows],
        dst_ref=buf.at[rows],
        send_sem=send_sems.at[tree, direction],
        recv_sem=recv_sems.at[tree, index],
        device_id=(row, neighbour(col, direction)),
        device_id_type=MESH,
    )


def bit(mask, col):
    return (jnp.int32(signed(mask)) >> col) & 1


def depth_of(tree, col):
    return sum(bit(mask, col) << b for b, mask in enumerate(DEPTHS[tree]))


def tree_forward(buf, send_sems, recv_sems, step, count, piece, depths, col):
    for tree in range(4):
        index = step - LAG * depths[tree]
        rows = pl.ds(pl.multiple_of((index * 4 + tree) * piece, piece), piece)

        @pl.when((index >= 0) & (index < count))
        def _():
            @pl.when(col != 0)
            def _():
                pltpu.make_async_copy(buf.at[rows], buf.at[rows], recv_sems.at[tree, index]).wait()

            for direction in range(4):

                @pl.when(passes(tree, direction, col))
                def _():
                    tree_send(buf, send_sems, recv_sems, tree, direction, index, rows, col).start()


def tree_drain(buf, send_sems, recv_sems, total, col):
    for tree in range(4):
        for direction in range(4):

            @pl.when(passes(tree, direction, col))
            def _():
                tree_send(
                    buf, send_sems, recv_sems, tree, direction, 0, pl.ds(0, total), col
                ).wait_send()


def gather_kernel(
    a_hbm,
    p_hbm,
    g_out,
    top_out,
    a,
    p,
    part,
    slots,
    total,
    top,
    tree_sends,
    tree_recvs,
    rs_sends,
    rs_recvs,
    ag_sends,
    ag_recvs,
    top_sends,
    top_recv,
    local_sems,
):
    row, col = lax.axis_index("row"), lax.axis_index("col")
    rows, width = a.shape
    share = PANEL // ROW
    macro = PANEL
    count = rows // macro
    per_macro = macro // (4 * PIECE)

    panel_copy = pltpu.make_async_copy(a_hbm.at[:, pl.ds(0, PANEL)], p, local_sems.at[0])
    loads = [
        pltpu.make_async_copy(
            a_hbm.at[pl.ds(i * PANEL, PANEL)], a.at[pl.ds(i * PANEL, PANEL)], local_sems.at[1 + i]
        )
        for i in range(count)
    ]

    @pl.when(col == 0)
    def _():
        panel_copy.start()

    for load in loads:
        load.start()

    barrier = pltpu.get_barrier_semaphore()
    peers = [lax.rem(row + d, ROW) for d in range(1, ROW)]
    for peer in peers:
        pl.semaphore_signal(barrier, inc=1, device_id=(peer, col), device_id_type=MESH)
    for direction in range(4):
        pl.semaphore_signal(
            barrier, inc=1, device_id=(row, neighbour(col, direction)), device_id_type=MESH
        )
    pl.semaphore_wait(barrier, len(peers) + 4)

    def top_copy(d):
        return pltpu.make_async_remote_copy(
            src_ref=a.at[pl.ds(0, PANEL)],
            dst_ref=top,
            send_sem=top_sends.at[d],
            recv_sem=top_recv,
            device_id=(peers[d], col),
            device_id_type=MESH,
        )

    loads[0].wait()

    @pl.when((row == 0) & (col != 0))
    def _():
        for d in range(ROW - 1):
            top_copy(d).start()

    @pl.when(col == 0)
    def _():
        panel_copy.wait()

    for load in loads[1:]:
        load.wait()

    part[...] = jnp.zeros_like(part)

    depths = [depth_of(tree, col) for tree in range(4)]
    deepest = functools.reduce(jnp.maximum, depths)
    pieces = count * per_macro

    @pl.loop(0, pieces + LAG * deepest)
    def _(step):
        tree_forward(p, tree_sends, tree_recvs, step, pieces, PIECE, depths, col)
        due = step - LAG * deepest + 1

        @pl.when((due > 0) & (lax.rem(due, per_macro) == 0))
        def _():
            i = lax.div(due, per_macro) - 1
            block = pl.ds(pl.multiple_of(i * macro, macro), macro)
            part[...] += dot_t(p[block], a[block])
            pltpu.make_async_copy(p.at[block], p_hbm.at[block], local_sems.at[0]).start()

    def part_copy(d):
        return pltpu.make_async_remote_copy(
            src_ref=part.at[pl.ds(pl.multiple_of(peers[d] * share, share), share)],
            dst_ref=slots.at[d],
            send_sem=rs_sends.at[d],
            recv_sem=rs_recvs.at[d],
            device_id=(peers[d], col),
            device_id_type=MESH,
        )

    mine = pl.ds(pl.multiple_of(row * share, share), share)

    def sum_copy(d):
        return pltpu.make_async_remote_copy(
            src_ref=total.at[mine],
            dst_ref=total.at[mine],
            send_sem=ag_sends.at[d],
            recv_sem=ag_recvs.at[d],
            device_id=(peers[d], col),
            device_id_type=MESH,
        )

    for d in range(ROW - 1):
        part_copy(d).start()

    @pl.when((row == 0) & (col == 0))
    def _():
        for d in range(ROW - 1):
            top_copy(d).start()

    acc = part[mine]
    for d in range(ROW - 1):
        part_copy(d).wait_recv()
        acc += slots[d]
    total[mine] = acc
    for d in range(ROW - 1):
        sum_copy(d).start()
    for d in range(ROW - 1):
        sum_copy(d).wait_recv()
    g_out[...] = total[...]

    @pl.when(row != 0)
    def _():
        top_copy(0).wait_recv()
        top_out[...] = top[...]

    @pl.when(row == 0)
    def _():
        top_out[...] = a[pl.ds(0, PANEL)]
        for d in range(ROW - 1):
            top_copy(d).wait_send()

    for d in range(ROW - 1):
        part_copy(d).wait_send()
        sum_copy(d).wait_send()
    tree_drain(p, tree_sends, tree_recvs, rows // 4, col)
    pltpu.make_async_copy(p, p_hbm, local_sems.at[0]).wait()


def gather(matrix):
    rows, width = matrix.shape
    count = rows // PANEL
    dma = pltpu.SemaphoreType.DMA
    return pl.pallas_call(
        gather_kernel,
        name="gather",
        out_shape=(
            jax.ShapeDtypeStruct((rows, PANEL), jnp.float32),
            jax.ShapeDtypeStruct((PANEL, width), jnp.float32),
            jax.ShapeDtypeStruct((PANEL, width), jnp.float32),
        ),
        in_specs=[pl.BlockSpec(memory_space=pl.ANY)],
        out_specs=(
            pl.BlockSpec(memory_space=pl.ANY),
            pl.BlockSpec(memory_space=pltpu.VMEM),
            pl.BlockSpec(memory_space=pltpu.VMEM),
        ),
        scratch_shapes=[
            pltpu.VMEM((rows, width), jnp.float32),
            pltpu.VMEM((rows, PANEL), jnp.float32),
            pltpu.VMEM((PANEL, width), jnp.float32),
            pltpu.VMEM((ROW - 1, PANEL // ROW, width), jnp.float32),
            pltpu.VMEM((PANEL, width), jnp.float32),
            pltpu.VMEM((PANEL, width), jnp.float32),
            dma((4, 4)),
            dma((4, rows // (4 * PIECE))),
            dma((ROW - 1,)),
            dma((ROW - 1,)),
            dma((ROW - 1,)),
            dma((ROW - 1,)),
            dma((ROW - 1,)),
            dma(()),
            dma((1 + count,)),
        ],
        compiler_params=pltpu.CompilerParams(
            collective_id=0, has_side_effects=True, vmem_limit_bytes=48 << 20
        ),
    )(matrix)


def eliminate(block, full):
    size, width = block.shape
    index = lax.broadcasted_iota(jnp.int32, (size, 1), 0)
    pivots = jnp.zeros((size, 1), jnp.float32)
    for k in range(size):
        column = block[:, k : k + 1]
        row = block[k : k + 1, :]
        pivot = block[k : k + 1, k : k + 1]
        keep = index != k if full else index > k
        factor = jnp.where(keep, column, 0.0) * (1.0 / pivot)
        pivots = jnp.where(index == k, pivot, pivots)
        block = block - factor * row
    return block, pivots


def factor_kernel(g, top, out, chol, gj):
    @pl.when(lax.axis_index("col") == 0)
    def _():
        b = BLOCK
        blocks = PANEL // b
        eye = jnp.eye(b, dtype=jnp.float32)
        chol[...] = jnp.zeros_like(chol)
        gj[...] = jnp.zeros_like(gj)

        def chol_block(j):
            lo, hi = j * b, (j + 1) * b
            sym = g[lo:hi, :PANEL]
            if j == 0:
                left, right = sym, None
            else:
                prod = dot_t(chol[:lo, lo:hi], chol[:lo, :])
                left, right = sym - prod[:, :PANEL], -prod[:, PANEL : PANEL + lo]
            done, pivots = eliminate(jnp.concatenate([left[:, lo:hi], eye], axis=1), False)
            inv = done[:, b:] * lax.rsqrt(pivots)
            parts = [left[:, lo:]]
            if right is not None:
                parts.append(right)
            parts.append(eye)
            res = dot(inv, jnp.concatenate(parts, axis=1))
            chol[lo:hi, lo : PANEL + hi] = res

        def gj_block(j):
            lo, hi = j * b, (j + 1) * b
            rowk = chol[lo:hi, :PANEL] + top[lo:hi, :PANEL]
            if j == 0:
                work = rowk
                right = None
            else:
                prod = dot(rowk[:, :lo], gj[:lo, :])
                work = rowk - prod[:, :PANEL]
                right = -prod[:, PANEL : PANEL + lo]
            done, pivots = eliminate(jnp.concatenate([work[:, lo:hi], eye], axis=1), True)
            inv = done[:, b:] * (1.0 / pivots)
            parts = [work[:, lo:]]
            if right is not None:
                parts.append(right)
            parts.append(eye)
            new = dot(inv, jnp.concatenate(parts, axis=1))
            if j > 0:
                gj[:lo, lo : PANEL + hi] -= dot(gj[:lo, lo:hi], new)
            gj[lo:hi, lo : PANEL + hi] = new

        for step in range(blocks + 1):
            if step < blocks:
                chol_block(step)
            if step > 0:
                gj_block(step - 1)
        out[:PANEL] = chol[:, PANEL:]
        out[PANEL:] = gj[:, PANEL:]


def factor(g, top):
    vmem = pl.BlockSpec(memory_space=pltpu.VMEM)
    return pl.pallas_call(
        factor_kernel,
        name="factor",
        out_shape=jax.ShapeDtypeStruct((2 * PANEL, PANEL), jnp.float32),
        in_specs=[vmem, vmem],
        out_specs=vmem,
        scratch_shapes=[
            pltpu.VMEM((PANEL, 2 * PANEL), jnp.float32),
            pltpu.VMEM((PANEL, 2 * PANEL), jnp.float32),
        ],
    )(g, top)


SMALL = 16


def spread_kernel(f_hbm, g, top, z_out, x_out, f, tree_sends, tree_recvs, local_sem):
    row, col = lax.axis_index("row"), lax.axis_index("col")
    load = pltpu.make_async_copy(f_hbm, f, local_sem)

    @pl.when(col == 0)
    def _():
        load.start()

    barrier = pltpu.get_barrier_semaphore()
    for direction in range(4):
        pl.semaphore_signal(
            barrier, inc=1, device_id=(row, neighbour(col, direction)), device_id_type=MESH
        )
    pl.semaphore_wait(barrier, 4)

    @pl.when(col == 0)
    def _():
        load.wait()

    count = 2 * PANEL // (4 * SMALL)
    depths = [depth_of(tree, col) for tree in range(4)]
    deepest = functools.reduce(jnp.maximum, depths)

    @pl.loop(0, count + LAG * deepest)
    def _(step):
        tree_forward(f, tree_sends, tree_recvs, step, count, SMALL, depths, col)

    z = dot(f[:PANEL], g[...])
    z_out[...] = z
    x_out[...] = dot(f[PANEL:], z + top[...])
    tree_drain(f, tree_sends, tree_recvs, 2 * PANEL // 4, col)


def spread(factors, g, top):
    vmem = pl.BlockSpec(memory_space=pltpu.VMEM)
    dma = pltpu.SemaphoreType.DMA
    shape = jax.ShapeDtypeStruct(g.shape, jnp.float32)
    return pl.pallas_call(
        spread_kernel,
        name="spread",
        out_shape=(shape, shape),
        in_specs=[pl.BlockSpec(memory_space=pl.ANY), vmem, vmem],
        out_specs=(vmem, vmem),
        scratch_shapes=[
            pltpu.VMEM((2 * PANEL, PANEL), jnp.float32),
            dma((4, 4)),
            dma((4, 2 * PANEL // (4 * SMALL))),
            dma(()),
        ],
        compiler_params=pltpu.CompilerParams(collective_id=1, has_side_effects=True),
    )(factors, g, top)


TILE = 512


def update_kernel(a, p, z, x, out):
    out[...] = a[...] - dot(p[...], x[...])

    @pl.when((lax.axis_index("row") == 0) & (pl.program_id(0) == 0))
    def _():
        out[:PANEL] = -z[...]


def update(matrix, panel, z, x):
    rows, width = matrix.shape
    whole = pl.BlockSpec((PANEL, width), lambda i: (0, 0))
    return pl.pallas_call(
        update_kernel,
        name="update",
        out_shape=jax.ShapeDtypeStruct(matrix.shape, jnp.float32),
        grid=(rows // TILE,),
        in_specs=[
            pl.BlockSpec((TILE, width), lambda i: (i, 0)),
            pl.BlockSpec((TILE, PANEL), lambda i: (i, 0)),
            whole,
            whole,
        ],
        out_specs=pl.BlockSpec((TILE, width), lambda i: (i, 0)),
    )(matrix, panel, z, x)


def on_device(matrix):
    panel, g, top = gather(matrix)
    factors = factor(g, top)
    z, x = spread(factors, g, top)
    return update(matrix, panel, z, x)


def solution(mesh):
    in_specs = (P("row", "col"),)
    out_specs = P("row", "col")
    return jax.shard_map(
        on_device, mesh=mesh, in_specs=in_specs, out_specs=out_specs, check_vma=False
    )
```

time: 593 us -> 135 us (0.23); the launches traced: 583 us -> 134 us
  waiting for transfers between devices: 270 us -> 0 us
  other arithmetic: 220 us -> 0 us
  Pallas kernels: 0 us -> 130 us
  matrix products: 48.8 us -> 0 us
  between operations: 20.2 us -> 0.03 us
  local copies, waits for them, and re-layouts: 18.1 us -> 3.15 us
    psum x3 -> x0, waiting for transfers between devices: 260 us -> none  [the longest x2 226 us: broadcast(): return lax.psum(kept, axis)]
    another operation x39 -> x0, other arithmetic: 215 us -> none  [the longest x27 138 us: upper_of(): return jnp.linalg.cholesky(gram).T]
    pallas_call x0 -> x4, Pallas kernels: none -> 130 us  [the longest x1 63.4 us: gather(): pl.pallas_call(gather_kernel, name='gather', out_shape=(jax.ShapeDtypeStr...]
    dot_general x11 -> x0, matrix products: 30.2 us -> none  [the longest x1 8.37 us: on_device(): return matrix - jnp.dot(vectors, coeffs, precision=HIGHEST)]
    another operation x19 -> x0, matrix products: 18.7 us -> none  [the longest x3 10.9 us: apply_inverse(): return jax.scipy.linalg.solve_triangular(upper.T, rows.T, lower=True).T]
    another operation x24 -> x0, local copies, waits for them, and re-layouts: 10 us -> none
    ppermute x3 -> x0, waiting for transfers between devices: 9.32 us -> none  [partner_2(): return lax.ppermute(block, axis, route)]
  transfers between devices with their start and end apart: 6 -> 0, of which waited for: 6 -> 0; matrix products, arithmetic and copies ran while one was open for 6% -> 0% of each run, Pallas kernels for 0% -> 0%
where the time goes in v1:
time: 135 us; the launch traced here: 134 us
  Pallas kernels  130 us (96%)
  local copies, waits for them, and re-layouts  3.15 us (2%)
    pallas_call x1, Pallas kernels, gather(): pl.pallas_call(gather_kernel, name='gather', out_shape=(jax.ShapeDtypeStr...  63.4 us
    pallas_call x1, Pallas kernels, spread(): pl.pallas_call(spread_kernel, name='spread', out_shape=(shape, shape), in...  55.3 us
    pallas_call x1, Pallas kernels, update(): pl.pallas_call(update_kernel, name='update', out_shape=jax.ShapeDtypeStru...  9.79 us
    unnamed x6, local copies, waits for them, and re-layouts  3.15 us

profile of v1, /device:TPU:8, one launch (start us, length us, event | category | flops | bytes accessed | tf_op | source)
XLA Modules:
  0.0 133.6 jit_solution(14292045417642144706)
XLA Ops:
  0.0 63.4 %gather.1 = (f32[3072,256]{1,0:T(8,128)S(1)}, f32[256,384]{1,0:T(8,128)S(1)}, f32[256,384]{1,0:T(8,128)S(1)}) custom-call(f32[3072,384]{1,0:T(8,128)} %a.1), custom_call_target="tpu_custom_call" | custom-call | tf_op jit(solution)/shard_map/gather/pallas_call | solution.py:271
  63.4 0.0 copy-start
  63.4 1.6 %copy-done = f32[3072,256]{1,0:T(8,128)} copy-done((f32[3072,256]{1,0:T(8,128)}, f32[3072,256]{1,0:T(8,128)S(1)}, u32[]{:S(2)}) %copy-start) | copy-done | bytes 3145752
  65.0 0.0 copy-start.1
  65.0 0.7 copy-done.1
  65.8 0.0 copy-start.2
  65.8 0.8 copy-done.2
  66.6 1.9 %factor.1.f_hbm = f32[512,256]{1,0:T(8,128)} custom-call(f32[256,384]{1,0:T(8,128)} %copy-done.1, f32[256,384]{1,0:T(8,128)} %copy-done.2), custom_call_target="tpu_custom_call" | custom-call | tf_op jit(solution)/shard_map/factor/pallas_call | solution.py:381
  68.5 55.3 %spread.1 = (f32[256,384]{1,0:T(8,128)}, f32[256,384]{1,0:T(8,128)}) custom-call(f32[512,256]{1,0:T(8,128)} %factor.1.f_hbm, f32[256,384]{1,0:T(8,128)} %copy-done.1, f32[256,384]{1,0:T(8,128)} %copy-done.2), custom_call_target="tpu_custom_call" | custom-call | tf_op jit(solution)/shard_map/spread/pallas_call | solution.py:434
  123.8 9.8 %update.1 = f32[3072,384]{1,0:T(8,128)} custom-call(f32[3072,384]{1,0:T(8,128)} %a.1, f32[3072,256]{1,0:T(8,128)} %copy-done, f32[256,384]{1,0:T(8,128)} %get-tuple-element.13.z, f32[256,384]{1,0:T(8,128)} %get-tuple-element.14.x), custom_call_target="tpu_custom_call" | custom-call | tf_op jit(solution)/shard_map/update/pallas_call | solution.py:464
Async XLA Ops:
  63.4 1.6 %copy-start = (f32[3072,256]{1,0:T(8,128)}, f32[3072,256]{1,0:T(8,128)S(1)}, u32[]{:S(2)}) copy-start(f32[3072,256]{1,0:T(8,128)S(1)} %get-tuple-element.10.p) | copy-start | bytes 9437188
  65.0 0.7 copy-start.1
  65.8 0.8 copy-start.2

commit v2 on v1

--- a/solution.py
+++ b/solution.py
@@ -11,7 +11,7 @@
 Y, Z = 4, 8
 ROW = 8
 PIECE = 32
-BLOCK = 64
+BLOCK = 32
 MESH = pl.DeviceIdType.MESH
 HIGHEST = lax.Precision.HIGHEST
 
@@ -27,6 +27,7 @@
     (1515870810, 2381649390, 4294962692),
     (1515870810, 3474847550, 1693450230),
 )
+TOP_STEP = 8
 LAG = 4
 
 
@@ -57,6 +58,21 @@
     )
 
 
+def split2(x):
+    high = x.astype(jnp.bfloat16)
+    return high, (x - high.astype(jnp.float32)).astype(jnp.bfloat16)
+
+
+def dot_split(a, b):
+    a_high, a_low = split2(a)
+    b_high, b_low = split2(b)
+    return jnp.dot(
+        jnp.concatenate([a_high, a_low, a_high], axis=1),
+        jnp.concatenate([b_high, b_high, b_low], axis=0),
+        preferred_element_type=jnp.float32,
+    )
+
+
 def dot(a, b):
     return jnp.dot(a, b, precision=HIGHEST, preferred_element_type=jnp.float32)
 
@@ -81,9 +97,9 @@
     return sum(bit(mask, col) << b for b, mask in enumerate(DEPTHS[tree]))
 
 
-def tree_forward(buf, send_sems, recv_sems, step, count, piece, depths, col):
+def tree_forward(buf, send_sems, recv_sems, step, count, piece, lag, depths, col):
     for tree in range(4):
-        index = step - LAG * depths[tree]
+        index = step - lag * depths[tree]
         rows = pl.ds(pl.multiple_of((index * 4 + tree) * piece, piece), piece)
 
         @pl.when((index >= 0) & (index < count))
@@ -127,8 +143,10 @@
     rs_recvs,
     ag_sends,
     ag_recvs,
+    share_sends,
+    share_recv,
     top_sends,
-    top_recv,
+    top_recvs,
     local_sems,
 ):
     row, col = lax.axis_index("row"), lax.axis_index("col")
@@ -163,22 +181,38 @@
         )
     pl.semaphore_wait(barrier, len(peers) + 4)
 
+    mine = pl.ds(pl.multiple_of(row * share, share), share)
+
+    def share_copy(d):
+        theirs = pl.ds(pl.multiple_of(peers[d] * share, share), share)
+        return pltpu.make_async_remote_copy(
+            src_ref=a.at[theirs],
+            dst_ref=top.at[theirs],
+            send_sem=share_sends.at[d],
+            recv_sem=share_recv,
+            device_id=(peers[d], col),
+            device_id_type=MESH,
+        )
+
+    own_share = pltpu.make_async_copy(a.at[mine], top.at[mine], share_recv)
+
     def top_copy(d):
         return pltpu.make_async_remote_copy(
-            src_ref=a.at[pl.ds(0, PANEL)],
-            dst_ref=top,
+            src_ref=top.at[mine],
+            dst_ref=top.at[mine],
             send_sem=top_sends.at[d],
-            recv_sem=top_recv,
+            recv_sem=top_recvs.at[d],
             device_id=(peers[d], col),
             device_id_type=MESH,
         )
 
     loads[0].wait()
 
-    @pl.when((row == 0) & (col != 0))
-    def _():
+    @pl.when(row == 0)
+    def _():
+        own_share.start()
         for d in range(ROW - 1):
-            top_copy(d).start()
+            share_copy(d).start()
 
     @pl.when(col == 0)
     def _():
@@ -195,8 +229,14 @@
 
     @pl.loop(0, pieces + LAG * deepest)
     def _(step):
-        tree_forward(p, tree_sends, tree_recvs, step, pieces, PIECE, depths, col)
+        tree_forward(p, tree_sends, tree_recvs, step, pieces, PIECE, LAG, depths, col)
         due = step - LAG * deepest + 1
+
+        @pl.when(step == TOP_STEP)
+        def _():
+            own_share.wait()
+            for d in range(ROW - 1):
+                top_copy(d).start()
 
         @pl.when((due > 0) & (lax.rem(due, per_macro) == 0))
         def _():
@@ -215,8 +255,6 @@
             device_id_type=MESH,
         )
 
-    mine = pl.ds(pl.multiple_of(row * share, share), share)
-
     def sum_copy(d):
         return pltpu.make_async_remote_copy(
             src_ref=total.at[mine],
@@ -229,11 +267,6 @@
 
     for d in range(ROW - 1):
         part_copy(d).start()
-
-    @pl.when((row == 0) & (col == 0))
-    def _():
-        for d in range(ROW - 1):
-            top_copy(d).start()
 
     acc = part[mine]
     for d in range(ROW - 1):
@@ -246,16 +279,15 @@
         sum_copy(d).wait_recv()
     g_out[...] = total[...]
 
-    @pl.when(row != 0)
-    def _():
-        top_copy(0).wait_recv()
-        top_out[...] = top[...]
+    for d in range(ROW - 1):
+        top_copy(d).wait_recv()
+        top_copy(d).wait_send()
+    top_out[...] = top[...]
 
     @pl.when(row == 0)
     def _():
-        top_out[...] = a[pl.ds(0, PANEL)]
         for d in range(ROW - 1):
-            top_copy(d).wait_send()
+            share_copy(d).wait_send()
 
     for d in range(ROW - 1):
         part_copy(d).wait_send()
@@ -297,6 +329,8 @@
             dma((ROW - 1,)),
             dma((ROW - 1,)),
             dma(()),
+            dma((ROW - 1,)),
+            dma((ROW - 1,)),
             dma((1 + count,)),
         ],
         compiler_params=pltpu.CompilerParams(
@@ -305,19 +339,62 @@
     )(matrix)
 
 
-def eliminate(block, full):
-    size, width = block.shape
-    index = lax.broadcasted_iota(jnp.int32, (size, 1), 0)
-    pivots = jnp.zeros((size, 1), jnp.float32)
-    for k in range(size):
-        column = block[:, k : k + 1]
-        row = block[k : k + 1, :]
-        pivot = block[k : k + 1, k : k + 1]
-        keep = index != k if full else index > k
-        factor = jnp.where(keep, column, 0.0) * (1.0 / pivot)
-        pivots = jnp.where(index == k, pivot, pivots)
-        block = block - factor * row
-    return block, pivots
+def invert_pair(one, two):
+    half = one.shape[0]
+    width = 128
+    spare = [jnp.zeros((8, width - 2 * half), jnp.float32)] if width > 2 * half else []
+    xs = [
+        jnp.concatenate([one[i : i + 8], two[i : i + 8]] + spare, axis=1)
+        for i in range(0, half, 8)
+    ]
+    lane = lax.broadcasted_iota(jnp.int32, (8, width), 1)
+    index = lax.broadcasted_iota(jnp.int32, (8, width), 0)
+    right = lane >= half
+    offset = lax.rem(lane, half)
+    base = lane - offset
+    right_row, offset_row = right[:1], offset[:1]
+
+    def column(x, k):
+        return jnp.take_along_axis(x, base + k, axis=1)
+
+    for k in range(0, half, 2):
+        home, s = k // 8, k % 8
+        c0 = [column(x, k) for x in xs]
+        c1 = [column(x, k + 1) for x in xs]
+        a, b = c0[home][s : s + 1], c1[home][s : s + 1]
+        c, d = c0[home][s + 1 : s + 2], c1[home][s + 1 : s + 2]
+        det = a * d - b * c
+        inv = 1.0 / det
+        in_pair = (offset == k) | (offset == k + 1)
+        first, second = offset_row == k, offset_row == k + 1
+        r0, r1 = xs[home][s : s + 1], xs[home][s + 1 : s + 2]
+        r0 = jnp.where(first, 1.0, jnp.where(second, 0.0, r0))
+        r1 = jnp.where(first, 0.0, jnp.where(second, 1.0, r1))
+        w0 = (d * r0 - b * r1) * inv
+        w1 = (a * r1 - c * r0) * inv
+        w0b, w1b = jnp.broadcast_to(w0, (8, width)), jnp.broadcast_to(w1, (8, width))
+        u0b, u1b = jnp.where(right, w0b, 0.0), jnp.where(right, w1b, 0.0)
+        clear = in_pair & right
+        ra = lax.rsqrt(a)
+        top = jnp.broadcast_to(jnp.where(right_row, w0, r0 * ra), (8, width))
+        low = jnp.broadcast_to(
+            w1 * jnp.where(right_row, 1.0, ra * jnp.sqrt(jnp.where(right_row, 1.0, det))),
+            (8, width),
+        )
+        for i, x in enumerate(xs):
+            if i < home:
+                new = jnp.where(clear, 0.0, x) - (c0[i] * u0b + c1[i] * u1b)
+            elif i > home:
+                new = jnp.where(in_pair, 0.0, x) - (c0[i] * w0b + c1[i] * w1b)
+            else:
+                moves = right | (index > s)
+                new = jnp.where(in_pair & moves, 0.0, x) - jnp.where(
+                    moves, c0[i] * w0b + c1[i] * w1b, 0.0
+                )
+                new = jnp.where(index == s, top, new)
+                new = jnp.where(index == s + 1, low, new)
+            xs[i] = new
+    return jnp.concatenate(xs, axis=0)
 
 
 def factor_kernel(g, top, out, chol, gj):
@@ -326,52 +403,43 @@
         b = BLOCK
         blocks = PANEL // b
         eye = jnp.eye(b, dtype=jnp.float32)
+        lower = lax.broadcasted_iota(jnp.int32, (b, b), 0) >= lax.broadcasted_iota(
+            jnp.int32, (b, b), 1
+        )
         chol[...] = jnp.zeros_like(chol)
         gj[...] = jnp.zeros_like(gj)
 
-        def chol_block(j):
-            lo, hi = j * b, (j + 1) * b
-            sym = g[lo:hi, :PANEL]
-            if j == 0:
-                left, right = sym, None
-            else:
-                prod = dot_t(chol[:lo, lo:hi], chol[:lo, :])
-                left, right = sym - prod[:, :PANEL], -prod[:, PANEL : PANEL + lo]
-            done, pivots = eliminate(jnp.concatenate([left[:, lo:hi], eye], axis=1), False)
-            inv = done[:, b:] * lax.rsqrt(pivots)
-            parts = [left[:, lo:]]
-            if right is not None:
-                parts.append(right)
-            parts.append(eye)
-            res = dot(inv, jnp.concatenate(parts, axis=1))
-            chol[lo:hi, lo : PANEL + hi] = res
-
-        def gj_block(j):
-            lo, hi = j * b, (j + 1) * b
-            rowk = chol[lo:hi, :PANEL] + top[lo:hi, :PANEL]
-            if j == 0:
-                work = rowk
-                right = None
-            else:
-                prod = dot(rowk[:, :lo], gj[:lo, :])
-                work = rowk - prod[:, :PANEL]
-                right = -prod[:, PANEL : PANEL + lo]
-            done, pivots = eliminate(jnp.concatenate([work[:, lo:hi], eye], axis=1), True)
-            inv = done[:, b:] * (1.0 / pivots)
-            parts = [work[:, lo:]]
-            if right is not None:
-                parts.append(right)
-            parts.append(eye)
-            new = dot(inv, jnp.concatenate(parts, axis=1))
-            if j > 0:
-                gj[:lo, lo : PANEL + hi] -= dot(gj[:lo, lo:hi], new)
-            gj[lo:hi, lo : PANEL + hi] = new
-
         for step in range(blocks + 1):
+            one, two = eye, eye
             if step < blocks:
-                chol_block(step)
+                lo, hi = step * b, (step + 1) * b
+                left = g[lo:hi, lo:PANEL]
+                wide = [left]
+                if step > 0:
+                    prod = dot_t(chol[:lo, lo:hi], chol[:lo, lo : PANEL + lo])
+                    left = left - prod[:, : PANEL - lo]
+                    wide = [left, -prod[:, PANEL - lo :]]
+                wide.append(eye)
+                one = left[:, :b]
             if step > 0:
-                gj_block(step - 1)
+                glo, ghi = (step - 1) * b, step * b
+                work = chol[glo:ghi, :PANEL] + top[glo:ghi, :PANEL]
+                gwide = [work]
+                if glo > 0:
+                    prod = dot(work[:, :glo], gj[:glo, glo : PANEL + glo])
+                    work = work[:, glo:] - prod[:, : PANEL - glo]
+                    gwide = [work, -prod[:, PANEL - glo :]]
+                gwide.append(eye)
+                two = work[:, :b]
+            both = invert_pair(one, two)
+            if step < blocks:
+                inv = jnp.where(lower, both[:, :b], 0.0)
+                chol[lo:hi, lo : PANEL + hi] = dot(inv, jnp.concatenate(wide, axis=1))
+            if step > 0:
+                new = dot(both[:, b : 2 * b], jnp.concatenate(gwide, axis=1))
+                if glo > 0:
+                    gj[:glo, glo : PANEL + ghi] -= dot(gj[:glo, glo:ghi], new)
+                gj[glo:ghi, glo : PANEL + ghi] = new
         out[:PANEL] = chol[:, PANEL:]
         out[PANEL:] = gj[:, PANEL:]
 
@@ -392,6 +460,7 @@
 
 
 SMALL = 16
+SMALL_LAG = 7
 
 
 def spread_kernel(f_hbm, g, top, z_out, x_out, f, tree_sends, tree_recvs, local_sem):
@@ -417,13 +486,13 @@
     depths = [depth_of(tree, col) for tree in range(4)]
     deepest = functools.reduce(jnp.maximum, depths)
 
-    @pl.loop(0, count + LAG * deepest)
+    @pl.loop(0, count + SMALL_LAG * deepest)
     def _(step):
-        tree_forward(f, tree_sends, tree_recvs, step, count, SMALL, depths, col)
-
-    z = dot(f[:PANEL], g[...])
+        tree_forward(f, tree_sends, tree_recvs, step, count, SMALL, SMALL_LAG, depths, col)
+
+    z = dot_split(f[:PANEL], g[...])
     z_out[...] = z
-    x_out[...] = dot(f[PANEL:], z + top[...])
+    x_out[...] = dot_split(f[PANEL:], z + top[...])
     tree_drain(f, tree_sends, tree_recvs, 2 * PANEL // 4, col)
 
 
@@ -451,7 +520,7 @@
 
 
 def update_kernel(a, p, z, x, out):
-    out[...] = a[...] - dot(p[...], x[...])
+    out[...] = a[...] - dot_split(p[...], x[...])
 
     @pl.when((lax.axis_index("row") == 0) & (pl.program_id(0) == 0))
     def _():

time: 135 us -> 105 us (0.78)
  Pallas kernels: 130 us -> 102 us
    pallas_call x1, Pallas kernels: 55.3 us -> 27.9 us  [spread(): pl.pallas_call(spread_kernel, name='spread', out_shape=(shape, shape), in...]
    pallas_call x1, Pallas kernels: 9.79 us -> 8.31 us  [update(): pl.pallas_call(update_kernel, name='update', out_shape=jax.ShapeDtypeStru...]
where the time goes in v2:
time: 105 us
  Pallas kernels  102 us (97%)
  local copies, waits for them, and re-layouts  3.15 us (3%)
    pallas_call x1, Pallas kernels, gather(): pl.pallas_call(gather_kernel, name='gather', out_shape=(jax.ShapeDtypeStr...  63.6 us
    pallas_call x1, Pallas kernels, spread(): pl.pallas_call(spread_kernel, name='spread', out_shape=(shape, shape), in...  27.9 us
    pallas_call x1, Pallas kernels, update(): pl.pallas_call(update_kernel, name='update', out_shape=jax.ShapeDtypeStru...  8.31 us
    unnamed x6, local copies, waits for them, and re-layouts  3.15 us

profile of v2, /device:TPU:8, one launch (start us, length us, event | category | flops | bytes accessed | tf_op | source)
XLA Modules:
  0.0 104.9 jit_solution(16804602328027026229)
XLA Ops:
  0.0 63.6 %gather.1 = (f32[3072,256]{1,0:T(8,128)S(1)}, f32[256,384]{1,0:T(8,128)S(1)}, f32[256,384]{1,0:T(8,128)S(1)}) custom-call(f32[3072,384]{1,0:T(8,128)} %a.1), custom_call_target="tpu_custom_call" | custom-call | tf_op jit(solution)/shard_map/gather/pallas_call | solution.py:303
  63.6 0.0 copy-start
  63.6 1.6 %copy-done = f32[3072,256]{1,0:T(8,128)} copy-done((f32[3072,256]{1,0:T(8,128)}, f32[3072,256]{1,0:T(8,128)S(1)}, u32[]{:S(2)}) %copy-start) | copy-done | bytes 3145752
  65.3 0.0 copy-start.1
  65.3 0.7 copy-done.1
  66.0 0.0 copy-start.2
  66.0 0.8 copy-done.2
  66.8 1.9 %factor.1.f_hbm = f32[512,256]{1,0:T(8,128)} custom-call(f32[256,384]{1,0:T(8,128)} %copy-done.1, f32[256,384]{1,0:T(8,128)} %copy-done.2), custom_call_target="tpu_custom_call" | custom-call | tf_op jit(solution)/shard_map/factor/pallas_call | solution.py:449
  68.7 27.9 %spread.1 = (f32[256,384]{1,0:T(8,128)}, f32[256,384]{1,0:T(8,128)}) custom-call(f32[512,256]{1,0:T(8,128)} %factor.1.f_hbm, f32[256,384]{1,0:T(8,128)} %copy-done.1, f32[256,384]{1,0:T(8,128)} %copy-done.2), custom_call_target="tpu_custom_call" | custom-call | tf_op jit(solution)/shard_map/spread/pallas_call | solution.py:503
  96.6 8.3 %update.1 = f32[3072,384]{1,0:T(8,128)} custom-call(f32[3072,384]{1,0:T(8,128)} %a.1, f32[3072,256]{1,0:T(8,128)} %copy-done, f32[256,384]{1,0:T(8,128)} %get-tuple-element.13.z, f32[256,384]{1,0:T(8,128)} %get-tuple-element.14.x), custom_call_target="tpu_custom_call" | custom-call | tf_op jit(solution)/shard_map/update/pallas_call | solution.py:533
Async XLA Ops:
  63.6 1.6 %copy-start = (f32[3072,256]{1,0:T(8,128)}, f32[3072,256]{1,0:T(8,128)S(1)}, u32[]{:S(2)}) copy-start(f32[3072,256]{1,0:T(8,128)S(1)} %get-tuple-element.10.p) | copy-start | bytes 9437188
  65.3 0.7 copy-start.1
  66.0 0.8 copy-start.2

commit v3 on v2

--- a/solution.py
+++ b/solution.py
@@ -12,6 +12,8 @@
 ROW = 8
 PIECE = 32
 BLOCK = 32
+SMALL = 32
+SMALL_LAG = 4
 MESH = pl.DeviceIdType.MESH
 HIGHEST = lax.Precision.HIGHEST
 
@@ -53,8 +55,9 @@
 
 
 def dot_t(a, b):
+    precision = HIGHEST if a.dtype == jnp.float32 else None
     return lax.dot_general(
-        a, b, (((0,), (0,)), ((), ())), precision=HIGHEST, preferred_element_type=jnp.float32
+        a, b, (((0,), (0,)), ((), ())), precision=precision, preferred_element_type=jnp.float32
     )
 
 
@@ -69,6 +72,17 @@
     return jnp.dot(
         jnp.concatenate([a_high, a_low, a_high], axis=1),
         jnp.concatenate([b_high, b_high, b_low], axis=0),
+        preferred_element_type=jnp.float32,
+    )
+
+
+def dot_t_split(a, b):
+    a_high, a_low = split2(a)
+    b_high, b_low = split2(b)
+    return lax.dot_general(
+        jnp.concatenate([a_high, a_low, a_high], axis=0),
+        jnp.concatenate([b_high, b_high, b_low], axis=0),
+        (((0,), (0,)), ((), ())),
         preferred_element_type=jnp.float32,
     )
 
@@ -126,11 +140,114 @@
                 ).wait_send()
 
 
+def invert_pair(one, two):
+    half = one.shape[0]
+    width = 128
+    spare = [jnp.zeros((8, width - 2 * half), jnp.float32)] if width > 2 * half else []
+    xs = [
+        jnp.concatenate([one[i : i + 8], two[i : i + 8]] + spare, axis=1)
+        for i in range(0, half, 8)
+    ]
+    lane = lax.broadcasted_iota(jnp.int32, (8, width), 1)
+    index = lax.broadcasted_iota(jnp.int32, (8, width), 0)
+    right = lane >= half
+    offset = lax.rem(lane, half)
+    base = lane - offset
+    right_row, offset_row = right[:1], offset[:1]
+
+    def column(x, k):
+        return jnp.take_along_axis(x, base + k, axis=1)
+
+    for k in range(0, half, 2):
+        home, s = k // 8, k % 8
+        c0 = [column(x, k) for x in xs]
+        c1 = [column(x, k + 1) for x in xs]
+        a, b = c0[home][s : s + 1], c1[home][s : s + 1]
+        c, d = c0[home][s + 1 : s + 2], c1[home][s + 1 : s + 2]
+        det = a * d - b * c
+        inv = 1.0 / det
+        in_pair = (offset == k) | (offset == k + 1)
+        first, second = offset_row == k, offset_row == k + 1
+        r0, r1 = xs[home][s : s + 1], xs[home][s + 1 : s + 2]
+        r0 = jnp.where(first, 1.0, jnp.where(second, 0.0, r0))
+        r1 = jnp.where(first, 0.0, jnp.where(second, 1.0, r1))
+        w0 = (d * r0 - b * r1) * inv
+        w1 = (a * r1 - c * r0) * inv
+        w0b, w1b = jnp.broadcast_to(w0, (8, width)), jnp.broadcast_to(w1, (8, width))
+        u0b, u1b = jnp.where(right, w0b, 0.0), jnp.where(right, w1b, 0.0)
+        clear = in_pair & right
+        ra = lax.rsqrt(a)
+        top = jnp.broadcast_to(jnp.where(right_row, w0, r0 * ra), (8, width))
+        low = jnp.broadcast_to(
+            w1 * jnp.where(right_row, 1.0, ra * jnp.sqrt(jnp.where(right_row, 1.0, det))),
+            (8, width),
+        )
+        for i, x in enumerate(xs):
+            if i < home:
+                new = jnp.where(clear, 0.0, x) - (c0[i] * u0b + c1[i] * u1b)
+            elif i > home:
+                new = jnp.where(in_pair, 0.0, x) - (c0[i] * w0b + c1[i] * w1b)
+            else:
+                moves = right | (index > s)
+                new = jnp.where(in_pair & moves, 0.0, x) - jnp.where(
+                    moves, c0[i] * w0b + c1[i] * w1b, 0.0
+                )
+                new = jnp.where(index == s, top, new)
+                new = jnp.where(index == s + 1, low, new)
+            xs[i] = new
+    return jnp.concatenate(xs, axis=0)
+
+
+def factor(g, top, out, chol, gj):
+    b = BLOCK
+    blocks = PANEL // b
+    eye = jnp.eye(b, dtype=jnp.float32)
+    lower = lax.broadcasted_iota(jnp.int32, (b, b), 0) >= lax.broadcasted_iota(
+        jnp.int32, (b, b), 1
+    )
+    chol[...] = jnp.zeros_like(chol)
+    gj[...] = jnp.zeros_like(gj)
+
+    for step in range(blocks + 1):
+        one, two = eye, eye
+        if step < blocks:
+            lo, hi = step * b, (step + 1) * b
+            left = g[lo:hi, lo:PANEL]
+            wide = [left]
+            if step > 0:
+                prod = dot_t(chol[:lo, lo:hi], chol[:lo, lo : PANEL + lo])
+                left = left - prod[:, : PANEL - lo]
+                wide = [left, -prod[:, PANEL - lo :]]
+            wide.append(eye)
+            one = left[:, :b]
+        if step > 0:
+            glo, ghi = (step - 1) * b, step * b
+            work = chol[glo:ghi, :PANEL] + top[glo:ghi, :PANEL]
+            gwide = [work]
+            if glo > 0:
+                prod = dot(work[:, :glo], gj[:glo, glo : PANEL + glo])
+                work = work[:, glo:] - prod[:, : PANEL - glo]
+                gwide = [work, -prod[:, PANEL - glo :]]
+            gwide.append(eye)
+            two = work[:, :b]
+        both = invert_pair(one, two)
+        if step < blocks:
+            inv = jnp.where(lower, both[:, :b], 0.0)
+            chol[lo:hi, lo : PANEL + hi] = dot(inv, jnp.concatenate(wide, axis=1))
+        if step > 0:
+            new = dot(both[:, b : 2 * b], jnp.concatenate(gwide, axis=1))
+            if glo > 0:
+                gj[:glo, glo : PANEL + ghi] -= dot(gj[:glo, glo:ghi], new)
+            gj[glo:ghi, glo : PANEL + ghi] = new
+    out[:PANEL] = chol[:, PANEL:]
+    out[PANEL:] = gj[:, PANEL:]
+
+
 def gather_kernel(
     a_hbm,
     p_hbm,
-    g_out,
-    top_out,
+    z_out,
+    x_out,
     a,
     p,
     part,
@@ -148,6 +265,12 @@
     top_sends,
     top_recvs,
     local_sems,
+    f,
+    chol,
+    gj,
+    f_sends,
+    f_recvs,
+    half,
 ):
     row, col = lax.axis_index("row"), lax.axis_index("col")
     rows, width = a.shape
@@ -222,6 +345,7 @@
         load.wait()
 
     part[...] = jnp.zeros_like(part)
+    half[...] = jnp.zeros_like(half)
 
     depths = [depth_of(tree, col) for tree in range(4)]
     deepest = functools.reduce(jnp.maximum, depths)
@@ -242,8 +366,29 @@
         def _():
             i = lax.div(due, per_macro) - 1
             block = pl.ds(pl.multiple_of(i * macro, macro), macro)
-            part[...] += dot_t(p[block], a[block])
+
+            @pl.when(col == 0)
+            def _():
+                high, low = split2(p[block])
+                rest = p[block] - high.astype(jnp.float32) - low.astype(jnp.float32)
+                part[:, :PANEL] += dot_t(
+                    jnp.concatenate([high, low], axis=0), jnp.concatenate([high, low], axis=0)
+                )
+                half[...] += dot_t(
+                    jnp.concatenate([high, high], axis=0),
+                    jnp.concatenate([low, rest.astype(jnp.bfloat16)], axis=0),
+                )
+                part[:, PANEL:] += dot_t_split(p[block], a[block, PANEL:])
+
+            @pl.when(col != 0)
+            def _():
+                part[...] += dot_t_split(p[block], a[block])
+
             pltpu.make_async_copy(p.at[block], p_hbm.at[block], local_sems.at[0]).start()
+
+    @pl.when(col == 0)
+    def _():
+        part[:, :PANEL] += half[...] + half[...].T
 
     def part_copy(d):
         return pltpu.make_async_remote_copy(
@@ -275,14 +420,34 @@
     total[mine] = acc
     for d in range(ROW - 1):
         sum_copy(d).start()
+
+
+    def sums_and_top():
+        for d in range(ROW - 1):
+            sum_copy(d).wait_recv()
+            top_copy(d).wait_recv()
+
+    @pl.when(col == 0)
+    def _():
+        sums_and_top()
+        factor(total, top, f, chol, gj)
+
+    small = 2 * PANEL // (4 * SMALL)
+
+    @pl.loop(0, small + SMALL_LAG * deepest)
+    def _(step):
+        tree_forward(f, f_sends, f_recvs, step, small, SMALL, SMALL_LAG, depths, col)
+
+    @pl.when(col != 0)
+    def _():
+        sums_and_top()
+
+    z = dot_split(f[:PANEL], total[...])
+    z_out[...] = z
+    x_out[...] = dot_split(f[PANEL:], z + top[...])
+
     for d in range(ROW - 1):
-        sum_copy(d).wait_recv()
-    g_out[...] = total[...]
-
-    for d in range(ROW - 1):
-        top_copy(d).wait_recv()
         top_copy(d).wait_send()
-    top_out[...] = top[...]
 
     @pl.when(row == 0)
     def _():
@@ -293,6 +458,7 @@
         part_copy(d).wait_send()
         sum_copy(d).wait_send()
     tree_drain(p, tree_sends, tree_recvs, rows // 4, col)
+    tree_drain(f, f_sends, f_recvs, 2 * PANEL // 4, col)
     pltpu.make_async_copy(p, p_hbm, local_sems.at[0]).wait()
 
 
@@ -332,188 +498,17 @@
             dma((ROW - 1,)),
             dma((ROW - 1,)),
             dma((1 + count,)),
+            pltpu.VMEM((2 * PANEL, PANEL), jnp.float32),
+            pltpu.VMEM((PANEL, 2 * PANEL), jnp.float32),
+            pltpu.VMEM((PANEL, 2 * PANEL), jnp.float32),
+            dma((4, 4)),
+            dma((4, 2 * PANEL // (4 * SMALL))),
+            pltpu.VMEM((PANEL, PANEL), jnp.float32),
         ],
         compiler_params=pltpu.CompilerParams(
             collective_id=0, has_side_effects=True, vmem_limit_bytes=48 << 20
         ),
     )(matrix)
-
-
-def invert_pair(one, two):
-    half = one.shape[0]
-    width = 128
-    spare = [jnp.zeros((8, width - 2 * half), jnp.float32)] if width > 2 * half else []
-    xs = [
-        jnp.concatenate([one[i : i + 8], two[i : i + 8]] + spare, axis=1)
-        for i in range(0, half, 8)
-    ]
-    lane = lax.broadcasted_iota(jnp.int32, (8, width), 1)
-    index = lax.broadcasted_iota(jnp.int32, (8, width), 0)
-    right = lane >= half
-    offset = lax.rem(lane, half)
-    base = lane - offset
-    right_row, offset_row = right[:1], offset[:1]
-
-    def column(x, k):
-        return jnp.take_along_axis(x, base + k, axis=1)
-
-    for k in range(0, half, 2):
-        home, s = k // 8, k % 8
-        c0 = [column(x, k) for x in xs]
-        c1 = [column(x, k + 1) for x in xs]
-        a, b = c0[home][s : s + 1], c1[home][s : s + 1]
-        c, d = c0[home][s + 1 : s + 2], c1[home][s + 1 : s + 2]
-        det = a * d - b * c
-        inv = 1.0 / det
-        in_pair = (offset == k) | (offset == k + 1)
-        first, second = offset_row == k, offset_row == k + 1
-        r0, r1 = xs[home][s : s + 1], xs[home][s + 1 : s + 2]
-        r0 = jnp.where(first, 1.0, jnp.where(second, 0.0, r0))
-        r1 = jnp.where(first, 0.0, jnp.where(second, 1.0, r1))
-        w0 = (d * r0 - b * r1) * inv
-        w1 = (a * r1 - c * r0) * inv
-        w0b, w1b = jnp.broadcast_to(w0, (8, width)), jnp.broadcast_to(w1, (8, width))
-        u0b, u1b = jnp.where(right, w0b, 0.0), jnp.where(right, w1b, 0.0)
-        clear = in_pair & right
-        ra = lax.rsqrt(a)
-        top = jnp.broadcast_to(jnp.where(right_row, w0, r0 * ra), (8, width))
-        low = jnp.broadcast_to(
-            w1 * jnp.where(right_row, 1.0, ra * jnp.sqrt(jnp.where(right_row, 1.0, det))),
-            (8, width),
-        )
-        for i, x in enumerate(xs):
-            if i < home:
-                new = jnp.where(clear, 0.0, x) - (c0[i] * u0b + c1[i] * u1b)
-            elif i > home:
-                new = jnp.where(in_pair, 0.0, x) - (c0[i] * w0b + c1[i] * w1b)
-            else:
-                moves = right | (index > s)
-                new = jnp.where(in_pair & moves, 0.0, x) - jnp.where(
-                    moves, c0[i] * w0b + c1[i] * w1b, 0.0
-                )
-                new = jnp.where(index == s, top, new)
-                new = jnp.where(index == s + 1, low, new)
-            xs[i] = new
-    return jnp.concatenate(xs, axis=0)
-
-
-def factor_kernel(g, top, out, chol, gj):
-    @pl.when(lax.axis_index("col") == 0)
-    def _():
-        b = BLOCK
-        blocks = PANEL // b
-        eye = jnp.eye(b, dtype=jnp.float32)
-        lower = lax.broadcasted_iota(jnp.int32, (b, b), 0) >= lax.broadcasted_iota(
-            jnp.int32, (b, b), 1
-        )
-        chol[...] = jnp.zeros_like(chol)
-        gj[...] = jnp.zeros_like(gj)
-
-        for step in range(blocks + 1):
-            one, two = eye, eye
-            if step < blocks:
-                lo, hi = step * b, (step + 1) * b
-                left = g[lo:hi, lo:PANEL]
-                wide = [left]
-                if step > 0:
-                    prod = dot_t(chol[:lo, lo:hi], chol[:lo, lo : PANEL + lo])
-                    left = left - prod[:, : PANEL - lo]
-                    wide = [left, -prod[:, PANEL - lo :]]
-                wide.append(eye)
-                one = left[:, :b]
-            if step > 0:
-                glo, ghi = (step - 1) * b, step * b
-                work = chol[glo:ghi, :PANEL] + top[glo:ghi, :PANEL]
-                gwide = [work]
-                if glo > 0:
-                    prod = dot(work[:, :glo], gj[:glo, glo : PANEL + glo])
-                    work = work[:, glo:] - prod[:, : PANEL - glo]
-                    gwide = [work, -prod[:, PANEL - glo :]]
-                gwide.append(eye)
-                two = work[:, :b]
-            both = invert_pair(one, two)
-            if step < blocks:
-                inv = jnp.where(lower, both[:, :b], 0.0)
-                chol[lo:hi, lo : PANEL + hi] = dot(inv, jnp.concatenate(wide, axis=1))
-            if step > 0:
-                new = dot(both[:, b : 2 * b], jnp.concatenate(gwide, axis=1))
-                if glo > 0:
-                    gj[:glo, glo : PANEL + ghi] -= dot(gj[:glo, glo:ghi], new)
-                gj[glo:ghi, glo : PANEL + ghi] = new
-        out[:PANEL] = chol[:, PANEL:]
-        out[PANEL:] = gj[:, PANEL:]
-
-
-def factor(g, top):
-    vmem = pl.BlockSpec(memory_space=pltpu.VMEM)
-    return pl.pallas_call(
-        factor_kernel,
-        name="factor",
-        out_shape=jax.ShapeDtypeStruct((2 * PANEL, PANEL), jnp.float32),
-        in_specs=[vmem, vmem],
-        out_specs=vmem,
-        scratch_shapes=[
-            pltpu.VMEM((PANEL, 2 * PANEL), jnp.float32),
-            pltpu.VMEM((PANEL, 2 * PANEL), jnp.float32),
-        ],
-    )(g, top)
-
-
-SMALL = 16
-SMALL_LAG = 7
-
-
-def spread_kernel(f_hbm, g, top, z_out, x_out, f, tree_sends, tree_recvs, local_sem):
-    row, col = lax.axis_index("row"), lax.axis_index("col")
-    load = pltpu.make_async_copy(f_hbm, f, local_sem)
-
-    @pl.when(col == 0)
-    def _():
-        load.start()
-
-    barrier = pltpu.get_barrier_semaphore()
-    for direction in range(4):
-        pl.semaphore_signal(
-            barrier, inc=1, device_id=(row, neighbour(col, direction)), device_id_type=MESH
-        )
-    pl.semaphore_wait(barrier, 4)
-
-    @pl.when(col == 0)
-    def _():
-        load.wait()
-
-    count = 2 * PANEL // (4 * SMALL)
-    depths = [depth_of(tree, col) for tree in range(4)]
-    deepest = functools.reduce(jnp.maximum, depths)
-
-    @pl.loop(0, count + SMALL_LAG * deepest)
-    def _(step):
-        tree_forward(f, tree_sends, tree_recvs, step, count, SMALL, SMALL_LAG, depths, col)
-
-    z = dot_split(f[:PANEL], g[...])
-    z_out[...] = z
-    x_out[...] = dot_split(f[PANEL:], z + top[...])
-    tree_drain(f, tree_sends, tree_recvs, 2 * PANEL // 4, col)
-
-
-def spread(factors, g, top):
-    vmem = pl.BlockSpec(memory_space=pltpu.VMEM)
-    dma = pltpu.SemaphoreType.DMA
-    shape = jax.ShapeDtypeStruct(g.shape, jnp.float32)
-    return pl.pallas_call(
-        spread_kernel,
-        name="spread",
-        out_shape=(shape, shape),
-        in_specs=[pl.BlockSpec(memory_space=pl.ANY), vmem, vmem],
-        out_specs=(vmem, vmem),
-        scratch_shapes=[
-            pltpu.VMEM((2 * PANEL, PANEL), jnp.float32),
-            dma((4, 4)),
-            dma((4, 2 * PANEL // (4 * SMALL))),
-            dma(()),
-        ],
-        compiler_params=pltpu.CompilerParams(collective_id=1, has_side_effects=True),
-    )(factors, g, top)
 
 
 TILE = 512
@@ -546,9 +541,7 @@
 
 
 def on_device(matrix):
-    panel, g, top = gather(matrix)
-    factors = factor(g, top)
-    z, x = spread(factors, g, top)
+    panel, z, x = gather(matrix)
     return update(matrix, panel, z, x)
 
 

time: 105 us -> 91.2 us (0.87)
  Pallas kernels: 102 us -> 87.9 us
    pallas_call x2 -> x0, Pallas kernels: 29.8 us -> none  [the longest x1 27.9 us: spread(): pl.pallas_call(spread_kernel, name='spread', out_shape=(shape, shape), in...]
    pallas_call x1, Pallas kernels: 63.6 us -> 79.6 us  [gather(): pl.pallas_call(gather_kernel, name='gather', out_shape=(jax.ShapeDtypeStr...]
where the time goes in v3:
time: 91.2 us; the launch traced here: 91 us
  Pallas kernels  87.9 us (96%)
  local copies, waits for them, and re-layouts  3.13 us (3%)
    pallas_call x1, Pallas kernels, gather(): pl.pallas_call(gather_kernel, name='gather', out_shape=(jax.ShapeDtypeStr...  79.6 us
    pallas_call x1, Pallas kernels, update(): pl.pallas_call(update_kernel, name='update', out_shape=jax.ShapeDtypeStru...  8.29 us
    unnamed x6, local copies, waits for them, and re-layouts  3.13 us

profile of v3, /device:TPU:8, one launch (start us, length us, event | category | flops | bytes accessed | tf_op | source)
XLA Modules:
  0.0 91.0 jit_solution(10642448037239043635)
XLA Ops:
  0.0 79.6 %gather.1 = (f32[3072,256]{1,0:T(8,128)S(1)}, f32[256,384]{1,0:T(8,128)S(1)}, f32[256,384]{1,0:T(8,128)S(1)}) custom-call(f32[3072,384]{1,0:T(8,128)} %a.1), custom_call_target="tpu_custom_call" | custom-call | tf_op jit(solution)/shard_map/gather/pallas_call | solution.py:469
  79.6 0.0 copy-start
  79.6 1.6 %copy-done = f32[3072,256]{1,0:T(8,128)} copy-done((f32[3072,256]{1,0:T(8,128)}, f32[3072,256]{1,0:T(8,128)S(1)}, u32[]{:S(2)}) %copy-start) | copy-done | bytes 3145752
  81.2 0.0 copy-start.1
  81.2 0.7 copy-done.1
  82.0 0.0 copy-start.2
  82.0 0.7 copy-done.2
  82.7 8.3 %update.1 = f32[3072,384]{1,0:T(8,128)} custom-call(f32[3072,384]{1,0:T(8,128)} %a.1, f32[3072,256]{1,0:T(8,128)} %copy-done, f32[256,384]{1,0:T(8,128)} %copy-done.1, f32[256,384]{1,0:T(8,128)} %copy-done.2), custom_call_target="tpu_custom_call" | custom-call | tf_op jit(solution)/shard_map/update/pallas_call | solution.py:528
Async XLA Ops:
  79.6 1.6 %copy-start = (f32[3072,256]{1,0:T(8,128)}, f32[3072,256]{1,0:T(8,128)S(1)}, u32[]{:S(2)}) copy-start(f32[3072,256]{1,0:T(8,128)S(1)} %get-tuple-element.8.p) | copy-start | bytes 9437188
  81.2 0.8 copy-start.1
  82.0 0.7 copy-start.2

commit v4 on v3

--- a/solution.py
+++ b/solution.py
@@ -511,7 +511,7 @@
     )(matrix)
 
 
-TILE = 512
+TILE = 1024
 
 
 def update_kernel(a, p, z, x, out):

time: 91.2 us -> 90.7 us (level)
  no operation moved by 1% of the time
where the time goes in v4:
time: 90.7 us; the launch traced here: 90.6 us
  Pallas kernels  87.5 us (96%)
  local copies, waits for them, and re-layouts  3.13 us (3%)
    pallas_call x1, Pallas kernels, gather(): pl.pallas_call(gather_kernel, name='gather', out_shape=(jax.ShapeDtypeStr...  79.6 us
    pallas_call x1, Pallas kernels, update(): pl.pallas_call(update_kernel, name='update', out_shape=jax.ShapeDtypeStru...  7.88 us
    unnamed x6, local copies, waits for them, and re-layouts  3.13 us

profile of v4, /device:TPU:8, one launch (start us, length us, event | category | flops | bytes accessed | tf_op | source)
XLA Modules:
  0.0 90.6 jit_solution(12996788859846764297)
XLA Ops:
  0.0 79.6 %gather.1 = (f32[3072,256]{1,0:T(8,128)S(1)}, f32[256,384]{1,0:T(8,128)S(1)}, f32[256,384]{1,0:T(8,128)S(1)}) custom-call(f32[3072,384]{1,0:T(8,128)} %a.1), custom_call_target="tpu_custom_call" | custom-call | tf_op jit(solution)/shard_map/gather/pallas_call | solution.py:469
  79.6 0.0 copy-start
  79.6 1.6 %copy-done = f32[3072,256]{1,0:T(8,128)} copy-done((f32[3072,256]{1,0:T(8,128)}, f32[3072,256]{1,0:T(8,128)S(1)}, u32[]{:S(2)}) %copy-start) | copy-done | bytes 3145752
  81.2 0.0 copy-start.1
  81.2 0.7 copy-done.1
  82.0 0.0 copy-start.2
  82.0 0.7 copy-done.2
  82.7 7.9 %update.1 = f32[3072,384]{1,0:T(8,128)} custom-call(f32[3072,384]{1,0:T(8,128)} %a.1, f32[3072,256]{1,0:T(8,128)} %copy-done, f32[256,384]{1,0:T(8,128)} %copy-done.1, f32[256,384]{1,0:T(8,128)} %copy-done.2), custom_call_target="tpu_custom_call" | custom-call | tf_op jit(solution)/shard_map/update/pallas_call | solution.py:528
Async XLA Ops:
  79.6 1.6 %copy-start = (f32[3072,256]{1,0:T(8,128)}, f32[3072,256]{1,0:T(8,128)S(1)}, u32[]{:S(2)}) copy-start(f32[3072,256]{1,0:T(8,128)S(1)} %get-tuple-element.8.p) | copy-start | bytes 9437188
  81.2 0.8 copy-start.1
  82.0 0.7 copy-start.2
